TPU v7x, 128 devices: a whole 4x4x4 slice. The times are simulated.
128 devices in a mesh: blk: 8 (over z, x_lo), tp: 16 (over x_hi, y, core).
Axes of the slice: x: 4 (x_hi: 2, x_lo: 2; x = x_hi * 2 + x_lo), y: 4, z: 4, core: 2. Of those that a mesh axis runs over, the one named last changes fastest.
Arguments:
- input_pool: bfloat16 [4096, 1792], P(None, 'tp'), may hold values from -6 to 6
- teacher_pool: bfloat16 [4096, 1792], P(None, 'tp'), may hold values from -6 to 6
- gate_weight: bfloat16 [1792, 9472], P(None, 'tp'), may hold values from -0.125 to 0.125
- up_weight: bfloat16 [1792, 9472], P(None, 'tp'), may hold values from -0.125 to 0.125
- params: float32 [8, 9472, 1792], P('blk', 'tp'), may hold values from -6 to 6
- batch_ids: int32 [8, 1024], replicated, may hold values from 0 to 4095
- cycle_order: int32 [8], replicated, may hold values from 0 to 7, each once
- edge_weight: float32 [8], replicated, may hold values from 0.1 to 0.45
Outputs:
- updated: float32 [8, 9472, 1792], P('blk', 'tp')
Inputs may be any that keep to these rules, and one draw needn't show every extreme that they name: `cycle_order`: the 8 cycle positions name 8 different agents.
All inputs are finite; a program needn't handle non-finite values.
Results may differ from a plain program's by a relative error of at most 0.0061.
Values may be sent and summed in bfloat16 or wider, within the bound.
No kernel may reach another device: no remote copies, remote signals or barrier semaphores. Data moves between devices by JAX's collectives and lax.ppermute only.
A program may use at most 128 MiB of HBM per device.

v0:
```python
import jax
import jax.numpy as jnp
from jax import lax
from jax.sharding import PartitionSpec as P


def rows_first(arrays, axis, dims):
    turned = [jnp.moveaxis(a, dim, 0) for a, dim in zip(arrays, dims)]
    both = jnp.concatenate([t.reshape(len(t), -1) for t in turned], axis=1)
    out, at, finished = (lax.all_gather(both, axis, axis=0, tiled=True), 0, [])
    for t, dim in zip(turned, dims):
        slab = out[:, at : at + t[0].size].reshape(-1, *t.shape[1:])
        finished.append(jnp.moveaxis(slab, 0, dim))
        at += t[0].size
    return tuple(finished)


def shifted(array, axis, by):
    count = lax.axis_size(axis)
    return lax.ppermute(array, axis, [(i, (i + by) % count) for i in range(count)])


def body(
    input_pool, teacher_pool, gate_weight, up_weight, params, batch_ids, cycle_order, edge_weight
):
    step_rate = 2.0
    groups = lax.axis_size("tp")
    place = lax.axis_index("blk")
    agents = cycle_order.shape[0]
    slots = jnp.arange(agents, dtype=jnp.int32)
    here = slots == place
    before = slots == (place + agents - 1) % agents
    agent = jnp.sum(jnp.where(here, cycle_order, 0))
    weight_next = jnp.sum(jnp.where(here, edge_weight, 0.0))
    weight_prev = jnp.sum(jnp.where(before, edge_weight, 0.0))
    weight_self = 1.0 - weight_next - weight_prev
    batch = lax.dynamic_slice_in_dim(batch_ids, agent, 1, 0)[0]
    inputs_local = jnp.take(input_pool, batch, axis=0)
    teacher_local = jnp.take(teacher_pool, batch, axis=0)
    hidden_dev = gate_weight.shape[1]
    scale = float(hidden_dev * groups) ** (-0.5)
    pieces = rows_first((inputs_local, teacher_local), "tp", (1, 1))
    rows = pieces[0]
    gate = jnp.dot(rows, gate_weight, preferred_element_type=jnp.float32)
    up = jnp.dot(rows, up_weight, preferred_element_type=jnp.float32)
    teacher = pieces[1]
    gate, up, teacher_full = (gate, up, teacher)
    hidden = (jax.nn.silu(gate) * up).astype(jnp.bfloat16)

    def gradient(weights):
        weights_half = weights.astype(jnp.bfloat16)
        partial_out = scale * jnp.dot(hidden, weights_half, preferred_element_type=jnp.float32)
        output = lax.psum(partial_out, "tp")
        resid = (output - teacher_full.astype(jnp.float32)).astype(jnp.bfloat16)
        return scale * lax.dot_general(
            hidden, resid, (((0,), (0,)), ((), ())), preferred_element_type=jnp.float32
        )

    start_field = params[0]
    grad_first = gradient(start_field)

    def mix_two(field):
        lower = shifted(field.astype(jnp.bfloat16), "blk", 1).astype(field.dtype)
        upper = shifted(field.astype(jnp.bfloat16), "blk", -1).astype(field.dtype)
        return weight_self * field + weight_next * upper + weight_prev * lower

    moved = mix_two(start_field) - step_rate * grad_first
    combined = moved - step_rate * grad_first
    grad_second = gradient(moved)
    result = mix_two(combined) - step_rate * (grad_second - grad_first)
    return result[None]


def solution(mesh):
    placed = (
        P(None, "tp"),
        P(None, "tp"),
        P(None, "tp"),
        P(None, "tp"),
        P("blk", "tp", None),
        P(),
        P(),
        P(),
    )
    return jax.shard_map(
        body, mesh=mesh, in_specs=placed, out_specs=P("blk", "tp", None), check_vma=False
    )
```

profile of v0, /device:TPU:0, one launch (start us, length us, event | category | flops | bytes accessed | tf_op | source)
XLA Modules:
  0.0 552.1 jit_solution(8042731751094256005)
XLA Ops:
  6.5 1.4 fusion.20
  9.9 0.8 constant_dynamic-slice_fusion
  10.7 2.3 copy.11
  13.0 1.6 copy.12
  14.6 4.2 gather_fusion
  18.8 4.3 gather_fusion.1
  23.1 1.2 select_bitcast_fusion.1
  24.3 0.1 pad_maximum_fusion
  24.4 1.0 copy.13
  25.4 0.0 all-gather.2.cloned.1.call-update
  25.4 0.0 all-reduce.3.cloned.1.call-start
  25.5 3.7 convert_bitcast_fusion
  29.2 67.0 %all-gather.2.cloned.1.call-done = bf16[1792,2048]{1,0:T(8,128)(2,1)} async-done(((bf16[112,2048]{1,0:T(8,128)(2,1)}), bf16[1792,2048]{1,0:T(8,128)(2,1)}) %all-gather.2.cloned.1.call-update) | async-done | bytes 7340048 | tf_op jit(solution)/shard_map/all_gather | solution.py:10
  96.2 4.5 fusion.11
  100.7 0.2 copy-done.7
  101.0 2.6 multiply_convert_fusion
  103.5 5.2 convolution_multiply_fusion.1
  108.7 0.0 all-reduce.5.cloned.1.call-start
  108.8 3.0 collective-permute-start
  111.8 0.7 fusion.19
  113.8 65.8 %collective-permute-done = bf16[592,1792]{1,0:T(8,128)(2,1)S(1)} collective-permute-done((bf16[592,1792]{1,0:T(8,128)(2,1)}, bf16[592,1792]{1,0:T(8,128)(2,1)S(1)}, u32[]{:S(2)}, u32[]{:S(2)}) %collective-permute-start) | collective-permute-done | bytes 2121760 | tf_op jit(solution)/shard_map/ppermute | solution.py:20
  179.6 62.6 %collective-permute-done.1 = bf16[592,1792]{1,0:T(8,128)(2,1)} collective-permute-done((bf16[592,1792]{1,0:T(8,128)(2,1)}, bf16[592,1792]{1,0:T(8,128)(2,1)}, u32[]{:S(2)}, u32[]{:S(2)}) %collective-permute-start.1) | collective-permute-done | bytes 2121760 | tf_op jit(solution)/shard_map/ppermute | solution.py:20
  242.2 65.9 %all-reduce.3.cloned.1.call-done = f32[1024,1792]{0,1:T(8,128)} async-done(((f32[1024,1792]{0,1:T(8,128)}), f32[1024,1792]{0,1:T(8,128)}) %all-reduce.3.cloned.1.call-update) | async-done | bytes 7340048 | tf_op jit(solution)/shard_map/psum | solution.py:53
  308.1 13.2 %fusion.4 = (bf16[592,1792]{1,0:T(8,128)(2,1)}, f32[592,1792]{1,0:T(8,128)S(1)}, f32[592,1792]{1,0:T(8,128)}) fusion(bf16[592,1792]{1,0:T(8,128)(2,1)} %collective-permute-done.1, f32[]{:T(128)} %get-tuple-element.7, bf16[592,1792]{1,0:T(8,128)(2,1)S(1)} %collective-permute-done, f32[]{:T(128)} %get-tuple-element.6, f32[1,592,1792]{2,1,0:T(8,128)} %param.14, ...), kind=kOutput, calls=%fused_computation.13 | convolution fusion | flops 2189824000 | bytes 31319044 | tf_op jit(solution)/shard_map/dot_general | solution.py:55
  321.3 2.0 copy-done.2
  323.3 5.2 convolution_multiply_fusion
  328.5 0.0 all-reduce.5.cloned.1.call-update
  328.5 1.6 copy-done.3
  330.1 2.9 collective-permute-start.2
  333.0 197.4 %all-reduce.5.cloned.1.call-done = f32[1024,1792]{0,1:T(8,128)} async-done(((f32[1024,1792]{0,1:T(8,128)}), f32[1024,1792]{0,1:T(8,128)}) %all-reduce.5.cloned.1.call-update) | async-done | bytes 7340048 | tf_op jit(solution)/shard_map/psum | solution.py:53
  530.5 6.6 %fusion.5 = f32[592,1792]{1,0:T(8,128)S(1)} fusion(bf16[1024,592]{0,1:T(8,128)(2,1)S(1)} %multiply_convert_fusion, f32[1024,1792]{0,1:T(8,128)} %all-reduce.5.cloned.1.call-done, bf16[1792,2048]{1,0:T(8,128)(2,1)} %all-gather.2.cloned.1.call-done), kind=kOutput, calls=%fused_computation.14 | convolution fusion | flops 2178154496 | bytes 16465920 | tf_op jit(solution)/shard_map/dot_general | solution.py:55
  537.1 8.5 %subtract_bitcast_fusion = f32[1,592,1792]{2,1,0:T(8,128)} fusion(f32[592,1792]{1,0:T(8,128)} %get-tuple-element.12, f32[592,1792]{1,0:T(8,128)S(1)} %fusion.5, bf16[592,1792]{1,0:T(8,128)(2,1)} %collective-permute-done.3, bf16[592,1792]{1,0:T(8,128)(2,1)} %collective-permute-done.2, f32[592,1792]{1,0:T(8,128)} %copy-done.2, f32[]{:T(128)} %get-tuple-element.7, ...), kind=kLoop, calls=%fused_computation.11 | loop fusion | flops 14852096 | bytes 21217292 | tf_op jit(solution)/shard_map/broadcast_in_dim | solution.py:71
  (21 shorter events, 0.1 us)
Async XLA Ops:
  6.5 89.6 %copy-start = (bf16[1792,592]{0,1:T(8,128)(2,1)S(1)}, bf16[1792,592]{0,1:T(8,128)(2,1)}, u32[]{:S(2)}) copy-start(bf16[1792,592]{0,1:T(8,128)(2,1)} %param.12) | copy-start | bytes 6365188
  6.5 89.6 %all-gather.2.cloned.1.call-start = ((), (), s32[]{:S(2)}) async-start(), calls=%async_computation | async-start | bytes 7798784 | tf_op jit(solution)/shard_map/all_gather | solution.py:10
  25.4 282.7 %all-reduce.3.cloned.1.call-start = ((), (), s32[]{:S(2)}) async-start(), calls=%async_computation.1 | async-start | bytes 14680064 | tf_op jit(solution)/shard_map/psum | solution.py:53
  96.2 4.5 copy-start.5
  96.2 4.8 copy-start.7
  101.0 2.6 copy-start.4
  108.7 3.1 copy-start.6
  108.7 421.7 %all-reduce.5.cloned.1.call-start = ((), (), s32[]{:S(2)}) async-start(), calls=%async_computation.2 | async-start | bytes 14680064 | tf_op jit(solution)/shard_map/psum | solution.py:53
  108.8 70.8 %collective-permute-start = (bf16[592,1792]{1,0:T(8,128)(2,1)}, bf16[592,1792]{1,0:T(8,128)(2,1)S(1)}, u32[]{:S(2)}, u32[]{:S(2)}) collective-permute-start(bf16[592,1792]{1,0:T(8,128)(2,1)} %convert_bitcast_fusion), channel_id=1, source_target_pairs={{0,112},{16,0},{32,16},{48,32},{64,48},{80,64},{96,80},{112,96},{1... | collective-permute-start | bytes 6365192 | tf_op jit(solution)/shard_map/ppermute | solution.py:20
  111.8 130.4 %collective-permute-start.1 = (bf16[592,1792]{1,0:T(8,128)(2,1)}, bf16[592,1792]{1,0:T(8,128)(2,1)}, u32[]{:S(2)}, u32[]{:S(2)}) collective-permute-start(bf16[592,1792]{1,0:T(8,128)(2,1)} %convert_bitcast_fusion), channel_id=1, source_target_pairs={{0,16},{16,32},{32,48},{48,64},{64,80},{80,96},{96,112},{112,0},{1... | collective-permute-start | bytes 6365192 | tf_op jit(solution)/shard_map/ppermute | solution.py:20
  321.3 2.0 copy-start.2
  328.5 1.6 copy-start.3
  330.1 206.9 %collective-permute-start.2 = (bf16[592,1792]{1,0:T(8,128)(2,1)S(1)}, bf16[592,1792]{1,0:T(8,128)(2,1)}, u32[]{:S(2)}, u32[]{:S(2)}) collective-permute-start(bf16[592,1792]{1,0:T(8,128)(2,1)S(1)} %copy-done.3), channel_id=1, source_target_pairs={{0,112},{16,0},{32,16},{48,32},{64,48},{80,64},{96,80},{112,96},{1... | collective-permute-start | bytes 6365192 | tf_op jit(solution)/shard_map/ppermute | solution.py:20
  333.0 204.0 %collective-permute-start.3 = (bf16[592,1792]{1,0:T(8,128)(2,1)S(1)}, bf16[592,1792]{1,0:T(8,128)(2,1)}, u32[]{:S(2)}, u32[]{:S(2)}) collective-permute-start(bf16[592,1792]{1,0:T(8,128)(2,1)S(1)} %copy-done.3), channel_id=1, source_target_pairs={{0,16},{16,32},{32,48},{48,64},{64,80},{80,96},{96,112},{112,0},{1... | collective-permute-start | bytes 6365192 | tf_op jit(solution)/shard_map/ppermute | solution.py:20
  537.0 8.5 %copy-start.1 = (bf16[1792,592]{0,1:T(8,128)(2,1)S(1)}, bf16[1792,592]{0,1:T(8,128)(2,1)}, u32[]{:S(2)}) copy-start(bf16[1792,592]{0,1:T(8,128)(2,1)} %param.12) | copy-start | bytes 6365188
Sparse Core Ops, SparseCore 0:
  25.5 70.5 all-gather.1
  108.9 199.2 all-reduce.2
  328.6 201.7 all-reduce.4
where the time goes:
time: 553 us; the launch traced here: 552 us
  waiting for transfers between devices  459 us (83%)
  matrix products  37.1 us (7%)
  local copies, waits for them, and re-layouts  18 us (3%)
  between operations  16.5 us (3%)
  other arithmetic  15.6 us (3%)
  starting transfers between devices  6.06 us (1%)
    psum x2, waiting for transfers between devices, gradient(): output = lax.psum(partial_out, 'tp')  263 us
    ppermute x4, waiting for transfers between devices, shifted(): lax.ppermute(array, axis, [(i, (i + by) % count) for i in range(count)])  128 us
    all_gather x1, waiting for transfers between devices, rows_first(): out, at, finished = (lax.all_gather(both, axis, axis=0, tiled=True), 0, [])  67 us
    dot_general x2, matrix products, gradient(): lax.dot_general(hidden, resid, (((0,), (0,)), ((), ())), preferred_elemen...  19.7 us
  transfers between devices with their start and end apart: 7, of which 5 were waited for; matrix products, arithmetic and copies ran while one was open for 2% of the time, Pallas kernels for 0%

commit v1 on v0

--- a/solution.py
+++ b/solution.py
@@ -7,7 +7,14 @@
 def rows_first(arrays, axis, dims):
     turned = [jnp.moveaxis(a, dim, 0) for a, dim in zip(arrays, dims)]
     both = jnp.concatenate([t.reshape(len(t), -1) for t in turned], axis=1)
-    out, at, finished = (lax.all_gather(both, axis, axis=0, tiled=True), 0, [])
+    out, at, finished = (
+        jnp.concatenate(
+            lax.all_to_all(jnp.stack([both for _ in range(lax.axis_size(axis))]), axis, 0, 0),
+            axis=0,
+        ),
+        0,
+        [],
+    )
     for t, dim in zip(turned, dims):
         slab = out[:, at : at + t[0].size].reshape(-1, *t.shape[1:])
         finished.append(jnp.moveaxis(slab, 0, dim))

time: 553 us -> 610 us (1.10)
  waiting for transfers between devices: 459 us -> 504 us
  starting transfers between devices: 6.06 us -> 12.3 us
    all_to_all x0 -> x1, waiting for transfers between devices: none -> 101 us  [rows_first(): lax.all_to_all(jnp.stack([both for _ in range(lax.axis_size(axis))]), axi...]
    all_gather x1 -> x0, waiting for transfers between devices: 67 us -> none  [rows_first(): out, at, finished = (lax.all_gather(both, axis, axis=0, tiled=True), 0, [])]
    psum x2, waiting for transfers between devices: 263 us -> 274 us  [gradient(): output = lax.psum(partial_out, 'tp')]
    all_to_all x0 -> x1, starting transfers between devices: none -> 7.19 us  [rows_first(): lax.all_to_all(jnp.stack([both for _ in range(lax.axis_size(axis))]), axi...]
where the time goes in v1:
time: 610 us; the launch traced here: 609 us
  waiting for transfers between devices  504 us (83%)
  matrix products  39.3 us (6%)
  local copies, waits for them, and re-layouts  21 us (3%)
  between operations  16.7 us (3%)
  other arithmetic  15.5 us (3%)
  starting transfers between devices  12.3 us (2%)
    psum x2, waiting for transfers between devices, gradient(): output = lax.psum(partial_out, 'tp')  274 us
    ppermute x4, waiting for transfers between devices, shifted(): lax.ppermute(array, axis, [(i, (i + by) % count) for i in range(count)])  130 us
    all_to_all x1, waiting for transfers between devices, rows_first(): lax.all_to_all(jnp.stack([both for _ in range(lax.axis_size(axis))]), axi...  101 us
    dot_general x2, matrix products, gradient(): lax.dot_general(hidden, resid, (((0,), (0,)), ((), ())), preferred_elemen...  19.7 us
  transfers between devices with their start and end apart: 7, of which 5 were waited for; matrix products, arithmetic and copies ran while one was open for 2% of the time, Pallas kernels for 0%

profile of v1, /device:TPU:0, one launch (start us, length us, event | category | flops | bytes accessed | tf_op | source)
XLA Modules:
  0.0 609.1 jit_solution(6898746920318463987)
XLA Ops:
  6.5 1.4 fusion.20
  9.9 0.8 constant_dynamic-slice_fusion
  10.7 2.3 copy.9
  13.0 1.6 copy.10
  14.6 4.2 gather_fusion
  18.8 4.3 gather_fusion.1
  23.1 1.2 select_bitcast_fusion.1
  24.3 0.1 pad_maximum_fusion
  24.4 0.2 copy.11
  24.6 3.9 stack.2
  28.6 7.2 %all-to-all-start = ((bf16[16,112,2048]{2,1,0:T(8,128)(2,1)}), bf16[16,112,2048]{2,1,0:T(8,128)(2,1)}, u32[]{:S(2)}, u32[]{:S(2)}) async-start(bf16[16,112,2048]{2,1,0:T(8,128)(2,1)} %stack.2), calls=%async_computation | async-start | bytes 14680064 | tf_op jit(solution)/shard_map/all_to_all | solution.py:12
  35.8 0.0 all-reduce.3.cloned.1.call-start
  35.8 3.7 convert_bitcast_fusion
  39.6 100.5 %all-to-all-done = bf16[16,112,2048]{2,1,0:T(8,128)(2,1)} async-done(((bf16[16,112,2048]{2,1,0:T(8,128)(2,1)}), bf16[16,112,2048]{2,1,0:T(8,128)(2,1)}, u32[]{:S(2)}, u32[]{:S(2)}) %all-to-all-start) | async-done | bytes 7340064 | tf_op jit(solution)/shard_map/all_to_all | solution.py:12
  140.1 4.5 fusion.11
  144.7 4.8 multiply_convert_fusion
  149.5 5.2 convolution_multiply_fusion.1
  154.7 0.0 all-reduce.5.cloned.1.call-start
  154.7 0.1 collective-permute-start
  154.8 2.0 collective-permute-start.1
  156.8 0.7 fusion.19
  158.7 59.9 %collective-permute-done = bf16[592,1792]{1,0:T(8,128)(2,1)S(1)} collective-permute-done((bf16[592,1792]{1,0:T(8,128)(2,1)}, bf16[592,1792]{1,0:T(8,128)(2,1)S(1)}, u32[]{:S(2)}, u32[]{:S(2)}) %collective-permute-start) | collective-permute-done | bytes 2121760 | tf_op jit(solution)/shard_map/ppermute | solution.py:27
  218.7 70.0 %collective-permute-done.1 = bf16[592,1792]{1,0:T(8,128)(2,1)} collective-permute-done((bf16[592,1792]{1,0:T(8,128)(2,1)}, bf16[592,1792]{1,0:T(8,128)(2,1)}, u32[]{:S(2)}, u32[]{:S(2)}) %collective-permute-start.1) | collective-permute-done | bytes 2121760 | tf_op jit(solution)/shard_map/ppermute | solution.py:27
  288.6 76.3 %all-reduce.3.cloned.1.call-done = f32[1024,1792]{0,1:T(8,128)} async-done(((f32[1024,1792]{0,1:T(8,128)}), f32[1024,1792]{0,1:T(8,128)}) %all-reduce.3.cloned.1.call-update) | async-done | bytes 7340048 | tf_op jit(solution)/shard_map/psum | solution.py:60
  365.0 13.1 %fusion.4 = (bf16[592,1792]{1,0:T(8,128)(2,1)}, f32[592,1792]{1,0:T(8,128)S(1)}, f32[592,1792]{1,0:T(8,128)}) fusion(bf16[592,1792]{1,0:T(8,128)(2,1)} %collective-permute-done.1, f32[]{:T(128)} %get-tuple-element.7, bf16[592,1792]{1,0:T(8,128)(2,1)S(1)} %collective-permute-done, f32[]{:T(128)} %get-tuple-element.6, f32[1,592,1792]{2,1,0:T(8,128)} %param.14, ...), kind=kOutput, calls=%fused_computation.13 | convolution fusion | flops 2189824000 | bytes 31319044 | tf_op jit(solution)/shard_map/dot_general | solution.py:62
  378.1 2.0 copy-done.2
  380.1 5.2 convolution_multiply_fusion
  385.3 1.6 copy-done.3
  386.9 3.0 collective-permute-start.2
  389.8 197.4 %all-reduce.5.cloned.1.call-done = f32[1024,1792]{0,1:T(8,128)} async-done(((f32[1024,1792]{0,1:T(8,128)}), f32[1024,1792]{0,1:T(8,128)}) %all-reduce.5.cloned.1.call-update) | async-done | bytes 7340048 | tf_op jit(solution)/shard_map/psum | solution.py:60
  587.3 6.6 %fusion.5 = f32[592,1792]{1,0:T(8,128)S(1)} fusion(bf16[1024,592]{0,1:T(8,128)(2,1)S(1)} %multiply_convert_fusion, f32[1024,1792]{0,1:T(8,128)} %all-reduce.5.cloned.1.call-done, bf16[1792,2048]{1,0:T(8,128)(2,1)} %bitcast.5), kind=kOutput, calls=%fused_computation.14 | convolution fusion | flops 2178154496 | bytes 16465920 | tf_op jit(solution)/shard_map/dot_general | solution.py:62
  593.9 8.4 %subtract_bitcast_fusion = f32[1,592,1792]{2,1,0:T(8,128)} fusion(f32[592,1792]{1,0:T(8,128)} %get-tuple-element.12, f32[592,1792]{1,0:T(8,128)S(1)} %fusion.5, bf16[592,1792]{1,0:T(8,128)(2,1)} %collective-permute-done.3, bf16[592,1792]{1,0:T(8,128)(2,1)} %collective-permute-done.2, f32[592,1792]{1,0:T(8,128)} %copy-done.2, f32[]{:T(128)} %get-tuple-element.7, ...), kind=kLoop, calls=%fused_computation.11 | loop fusion | flops 14852096 | bytes 21217292 | tf_op jit(solution)/shard_map/broadcast_in_dim | solution.py:78
  (19 shorter events, 0.1 us)
Async XLA Ops:
  6.5 133.6 %copy-start = (bf16[1792,592]{0,1:T(8,128)(2,1)S(1)}, bf16[1792,592]{0,1:T(8,128)(2,1)}, u32[]{:S(2)}) copy-start(bf16[1792,592]{0,1:T(8,128)(2,1)} %param.12) | copy-start | bytes 6365188
  28.6 111.5 %all-to-all-start = ((bf16[16,112,2048]{2,1,0:T(8,128)(2,1)}), bf16[16,112,2048]{2,1,0:T(8,128)(2,1)}, u32[]{:S(2)}, u32[]{:S(2)}) async-start(bf16[16,112,2048]{2,1,0:T(8,128)(2,1)} %stack.2), calls=%async_computation | async-start | bytes 14680064 | tf_op jit(solution)/shard_map/all_to_all | solution.py:12
  35.8 329.2 %all-reduce.3.cloned.1.call-start = ((), (), s32[]{:S(2)}) async-start(), calls=%async_computation.1 | async-start | bytes 14680064 | tf_op jit(solution)/shard_map/psum | solution.py:60
  140.1 4.5 copy-start.6
  144.6 4.8 copy-start.4
  154.6 2.2 copy-start.5
  154.7 432.6 %all-reduce.5.cloned.1.call-start = ((), (), s32[]{:S(2)}) async-start(), calls=%async_computation.2 | async-start | bytes 14680064 | tf_op jit(solution)/shard_map/psum | solution.py:60
  154.7 63.9 %collective-permute-start = (bf16[592,1792]{1,0:T(8,128)(2,1)}, bf16[592,1792]{1,0:T(8,128)(2,1)S(1)}, u32[]{:S(2)}, u32[]{:S(2)}) collective-permute-start(bf16[592,1792]{1,0:T(8,128)(2,1)} %convert_bitcast_fusion), channel_id=1, source_target_pairs={{0,112},{16,0},{32,16},{48,32},{64,48},{80,64},{96,80},{112,96},{1... | collective-permute-start | bytes 6365192 | tf_op jit(solution)/shard_map/ppermute | solution.py:27
  154.8 133.8 %collective-permute-start.1 = (bf16[592,1792]{1,0:T(8,128)(2,1)}, bf16[592,1792]{1,0:T(8,128)(2,1)}, u32[]{:S(2)}, u32[]{:S(2)}) collective-permute-start(bf16[592,1792]{1,0:T(8,128)(2,1)} %convert_bitcast_fusion), channel_id=1, source_target_pairs={{0,16},{16,32},{32,48},{48,64},{64,80},{80,96},{96,112},{112,0},{1... | collective-permute-start | bytes 6365192 | tf_op jit(solution)/shard_map/ppermute | solution.py:27
  378.1 2.0 copy-start.2
  385.3 1.6 copy-start.3
  386.9 206.9 %collective-permute-start.2 = (bf16[592,1792]{1,0:T(8,128)(2,1)S(1)}, bf16[592,1792]{1,0:T(8,128)(2,1)}, u32[]{:S(2)}, u32[]{:S(2)}) collective-permute-start(bf16[592,1792]{1,0:T(8,128)(2,1)S(1)} %copy-done.3), channel_id=1, source_target_pairs={{0,112},{16,0},{32,16},{48,32},{64,48},{80,64},{96,80},{112,96},{1... | collective-permute-start | bytes 6365192 | tf_op jit(solution)/shard_map/ppermute | solution.py:27
  389.8 204.0 %collective-permute-start.3 = (bf16[592,1792]{1,0:T(8,128)(2,1)S(1)}, bf16[592,1792]{1,0:T(8,128)(2,1)}, u32[]{:S(2)}, u32[]{:S(2)}) collective-permute-start(bf16[592,1792]{1,0:T(8,128)(2,1)S(1)} %copy-done.3), channel_id=1, source_target_pairs={{0,16},{16,32},{32,48},{48,64},{64,80},{80,96},{96,112},{112,0},{1... | collective-permute-start | bytes 6365192 | tf_op jit(solution)/shard_map/ppermute | solution.py:27
  593.8 8.4 %copy-start.1 = (bf16[1792,592]{0,1:T(8,128)(2,1)S(1)}, bf16[1792,592]{0,1:T(8,128)(2,1)}, u32[]{:S(2)}) copy-start(bf16[1792,592]{0,1:T(8,128)(2,1)} %param.12) | copy-start | bytes 6365188
Sparse Core Ops, SparseCore 0:
  154.8 210.1 all-reduce.2
  385.4 201.7 all-reduce.4
